TPU v7x, 32 devices: a whole 2x2x4 slice. The times are simulated.
32 devices in a mesh: tp: 4 (over y, x), row: 4 (over z), col: 2 (over core).
Axes of the slice: x: 2, y: 2, z: 4, core: 2. Of those that a mesh axis runs over, the one named last changes fastest.
Arguments:
- hidden: bfloat16 [128, 14336], P('col', 'row'), may hold values from -6 to 6
- out_grad: bfloat16 [128, 4096], P(None, ('tp', 'row')), may hold values from -6 to 6
- basis_in: bfloat16 [14336, 4096], P(('row', 'col'), 'tp'), may hold values from -0.046875 to 0.046875
- basis_out: bfloat16 [4096, 1024], P(('tp', 'row'), 'col'), may hold values from -0.09375 to 0.09375
- eigen: float32 [4096, 1024], P(('tp', 'row'), 'col'), may hold values from 0.02 to 2
Outputs:
- precond: float32 [4096, 14336], P(('tp', 'col'), 'row')
All inputs are finite; a program needn't handle non-finite values.
Results may differ from a plain program's by a relative error of at most 0.024.
Values may be sent and summed in bfloat16 or wider, within the bound.
No kernel may reach another device: no remote copies, remote signals or barrier semaphores. Data moves between devices by JAX's collectives and lax.ppermute only.
A program may use at most 64 MiB of HBM per device.

v0:
```python
import jax
import jax.numpy as jnp
from jax import lax
from jax.sharding import PartitionSpec as P

damping = 0.01


def contract_rows(left, right):
    return lax.dot_general(
        left, right, (((0,), (0,)), ((), ())), preferred_element_type=jnp.float32
    )


def contract_cols(left, right):
    return lax.dot_general(
        left, right, (((1,), (1,)), ((), ())), preferred_element_type=jnp.float32
    )


def shards(hidden, out_grad, basis_in, basis_out, eigen):
    tp_count = lax.axis_size("tp")
    col_count = lax.axis_size("col")
    basis_block = lax.all_gather(basis_in, "col", axis=0, tiled=True)
    partial_in = jnp.dot(hidden, basis_block, preferred_element_type=jnp.float32)
    rotated_in = lax.psum_scatter(
        partial_in.astype(jnp.bfloat16), "row", scatter_dimension=1, tiled=True
    )
    rotated_in = lax.all_gather(rotated_in, "col", axis=0, tiled=True)
    queries = rotated_in.shape[0]
    partial_out = jnp.dot(out_grad, basis_out, preferred_element_type=jnp.float32)
    rotated_out = lax.psum(partial_out, ("tp", "row")).astype(jnp.bfloat16)
    coeff = contract_rows(rotated_in, rotated_out)
    scaled = (coeff / (queries * (eigen + damping))).astype(jnp.bfloat16)
    mixed_part = contract_cols(scaled, lax.all_gather(basis_out, ("tp", "row"), axis=0, tiled=True))
    depth = mixed_part.shape[0]
    width = mixed_part.shape[1]
    mixed_part = mixed_part.reshape(depth, tp_count, col_count, width // (tp_count * col_count))
    mixed = lax.psum_scatter(
        mixed_part.astype(jnp.bfloat16), "col", scatter_dimension=2, tiled=True
    ).astype(jnp.float32)
    mixed = mixed.reshape(depth, width // col_count).astype(jnp.bfloat16)
    mixed = lax.all_gather(mixed, "row", axis=0, tiled=True)
    return lax.psum_scatter(
        lax.dot_general(
            mixed, basis_block, (((0,), (1,)), ((), ())), preferred_element_type=jnp.float32
        ).astype(jnp.bfloat16),
        "tp",
        scatter_dimension=0,
        tiled=True,
    ).astype(jnp.float32)


def solution(mesh):
    placed = (
        P("col", "row"),
        P(None, ("tp", "row")),
        P(("row", "col"), "tp"),
        P(("tp", "row"), "col"),
        P(("tp", "row"), "col"),
    )
    return jax.shard_map(
        shards, mesh=mesh, in_specs=placed, out_specs=P(("tp", "col"), "row"), check_vma=False
    )
```

profile of v0, /device:TPU:0, one launch (start us, length us, event | category | flops | bytes accessed | tf_op | source)
XLA Modules:
  0.0 397.8 jit_solution(9604397828768367093)
XLA Ops:
  7.4 0.0 copy-start
  7.4 0.0 all-gather.4.cloned.1.call-start
  7.4 0.7 all-gather.4.cloned.1.call-update
  8.1 0.0 copy-start.1
  8.1 0.0 copy-start.2
  8.1 0.0 copy-start.3
  8.1 0.0 reduce-scatter.4.cloned.1.call-start
  8.2 22.6 %all-gather.4.cloned.1.call-done = bf16[3584,1024]{1,0:T(8,128)(2,1)} async-done(((bf16[1792,1024]{1,0:T(8,128)(2,1)}), bf16[3584,1024]{1,0:T(8,128)(2,1)}) %all-gather.4.cloned.1.call-update) | async-done | bytes 7340048 | tf_op jit(solution)/shard_map/all_gather | solution.py:24
  30.8 0.0 copy-done
  30.8 5.1 %convolution_convert_fusion.2 = bf16[64,1024]{1,0:T(8,128)(2,1)} fusion(bf16[64,3584]{1,0:T(8,128)(2,1)S(1)} %copy-done, bf16[3584,1024]{1,0:T(8,128)(2,1)} %all-gather.4.cloned.1.call-done), kind=kOutput, calls=%fused_computation.4 | convolution fusion | flops 469827584 | bytes 7929856 | tf_op jit(solution)/shard_map/dot_general | solution.py:25
  35.9 0.0 reduce-scatter.4.cloned.1.call-update
  35.9 0.0 all-gather.6.cloned.1.call-start
  36.0 0.5 all-gather.6.cloned.1.call-update
  36.5 0.0 reduce-scatter.6.cloned.1.call-start
  36.5 0.0 copy-done.1
  36.6 0.0 copy-done.2
  36.6 0.2 fusion.9
  36.8 85.1 %all-reduce.1 = bf16[128,512]{1,0:T(8,128)(2,1)S(1)} all-reduce(f32[128,512]{1,0:T(8,128)S(1)} %fusion.9), channel_id=1, replica_groups=mesh['tp'=4,'row'=4,'col'=2] {'tp','row'}, use_global_device_ids=true, to_apply=%region_1.0 | all-reduce | flops 65536 | bytes 393216 | tf_op jit(solution)/shard_map/psum | solution.py:32
  121.9 0.0 reduce-scatter.4.cloned.1.call-done
  121.9 2.1 all_gather.13
  124.0 0.0 all-gather.6.cloned.1.call-done
  124.0 0.0 copy-done.3
  124.0 4.9 %convolution_convert_fusion.1 = bf16[256,4096]{1,0:T(8,128)(2,1)} fusion(bf16[4096,512]{1,0:T(8,128)(2,1)} %all-gather.6.cloned.1.call-done, bf16[128,256]{1,0:T(8,128)(2,1)S(1)} %all_gather.13, f32[256,512]{1,0:T(8,128)S(1)} %copy-done.3, bf16[128,512]{1,0:T(8,128)(2,1)S(1)} %all-reduce.1), kind=kOutput, calls=%fused_computation.1 | convolution fusion | flops 1108869120 | bytes 7012352 | tf_op jit(solution)/shard_map/dot_general | solution.py:16
  128.9 3.3 convert_element_type.30
  132.2 4.1 %copy.6 = bf16[256,4,2,512]{0,3,1,2:T(8,128)(2,1)} copy(bf16[256,4,2,512]{3,2,1,0:T(2,128)(2,1)S(1)} %convert_element_type.30) | data formatting | bytes 4194304 | tf_op jit(solution)/shard_map/convert_element_type | solution.py:40
  136.3 0.0 reduce-scatter.6.cloned.1.call-update
  136.4 0.0 all-gather.8.cloned.1.call-start
  136.4 6.9 %reduce-scatter.6.cloned.1.call-done = bf16[256,4,1,512]{0,3,1,2:T(8,128)(2,1)} async-done(((bf16[256,4,2,512]{0,3,1,2:T(8,128)(2,1)}), bf16[256,4,1,512]{0,3,1,2:T(8,128)(2,1)}) %reduce-scatter.6.cloned.1.call-update) | async-done | bytes 1048592 | tf_op jit(solution)/shard_map/reduce_scatter | solution.py:39
  143.3 0.0 all-gather.8.cloned.1.call-update
  143.4 0.0 reduce-scatter.8.cloned.1.call-start
  143.4 83.2 %all-gather.8.cloned.1.call-done = bf16[1024,2048]{0,1:T(8,128)(2,1)} async-done(((bf16[256,2048]{0,1:T(8,128)(2,1)}), bf16[1024,2048]{0,1:T(8,128)(2,1)}) %all-gather.8.cloned.1.call-update) | async-done | bytes 4194320 | tf_op jit(solution)/shard_map/all_gather | solution.py:43
  226.6 22.0 %convolution_convert_fusion = bf16[2048,3584]{1,0:T(8,128)(2,1)} fusion(bf16[1024,2048]{0,1:T(8,128)(2,1)} %all-gather.8.cloned.1.call-done, bf16[3584,1024]{1,0:T(8,128)(2,1)} %all-gather.4.cloned.1.call-done), kind=kOutput, calls=%fused_computation | convolution fusion | flops 15039725568 | bytes 26214400 | tf_op jit(solution)/shard_map/dot_general | solution.py:45
  248.6 0.0 reduce-scatter.8.cloned.1.call-update
  248.7 135.9 %reduce-scatter.8.cloned.1.call-done = bf16[512,3584]{1,0:T(8,128)(2,1)} async-done(((bf16[2048,3584]{1,0:T(8,128)(2,1)}), bf16[512,3584]{1,0:T(8,128)(2,1)}) %reduce-scatter.8.cloned.1.call-update) | async-done | bytes 3670032 | tf_op jit(solution)/shard_map/reduce_scatter | solution.py:44
  384.6 6.0 %convert_element_type.33 = f32[512,3584]{1,0:T(8,128)} convert(bf16[512,3584]{1,0:T(8,128)(2,1)} %reduce-scatter.8.cloned.1.call-done) | non-fusion elementwise | flops 1835008 | bytes 11010048 | tf_op jit(solution)/shard_map/convert_element_type | solution.py:51
Async XLA Ops:
  7.4 23.4 %copy-start = (bf16[64,3584]{1,0:T(8,128)(2,1)S(1)}, bf16[64,3584]{1,0:T(8,128)(2,1)}, u32[]{:S(2)}) copy-start(bf16[64,3584]{1,0:T(8,128)(2,1)} %param.5) | copy-start | bytes 1376260
  7.4 23.4 %all-gather.4.cloned.1.call-start = ((), (), s32[]{:S(2)}) async-start(), calls=%async_computation.3 | async-start | bytes 11010048 | tf_op jit(solution)/shard_map/all_gather | solution.py:24
  8.1 28.5 %copy-start.1 = (bf16[256,512]{1,0:T(8,128)(2,1)S(1)}, bf16[256,512]{1,0:T(8,128)(2,1)}, u32[]{:S(2)}) copy-start(bf16[256,512]{1,0:T(8,128)(2,1)} %param.8) | copy-start | bytes 786436
  8.1 28.5 %copy-start.2 = (bf16[128,256]{1,0:T(8,128)(2,1)S(1)}, bf16[128,256]{1,0:T(8,128)(2,1)}, u32[]{:S(2)}) copy-start(bf16[128,256]{1,0:T(8,128)(2,1)} %param.6) | copy-start | bytes 196612
  8.1 115.9 %copy-start.3 = (f32[256,512]{1,0:T(8,128)S(1)}, f32[256,512]{1,0:T(8,128)}, u32[]{:S(2)}) copy-start(f32[256,512]{1,0:T(8,128)} %param.9) | copy-start | bytes 1572868
  8.1 113.8 %reduce-scatter.4.cloned.1.call-start = ((), (), s32[]{:S(2)}) async-start(), calls=%async_computation.4 | async-start | bytes 163840 | tf_op jit(solution)/shard_map/reduce_scatter | solution.py:26
  35.9 88.1 %all-gather.6.cloned.1.call-start = ((), (), s32[]{:S(2)}) async-start(), calls=%async_computation.5 | async-start | bytes 4456448 | tf_op jit(solution)/shard_map/all_gather | solution.py:35
  36.5 106.8 %reduce-scatter.6.cloned.1.call-start = ((), (), s32[]{:S(2)}) async-start(), calls=%async_computation.6 | async-start | bytes 3145728 | tf_op jit(solution)/shard_map/reduce_scatter | solution.py:39
  136.4 90.2 %all-gather.8.cloned.1.call-start = ((), (), s32[]{:S(2)}) async-start(), calls=%async_computation.7 | async-start | bytes 5242880 | tf_op jit(solution)/shard_map/all_gather | solution.py:43
  143.4 241.2 %reduce-scatter.8.cloned.1.call-start = ((), (), s32[]{:S(2)}) async-start(), calls=%async_computation.8 | async-start | bytes 18350080 | tf_op jit(solution)/shard_map/reduce_scatter | solution.py:44
Sparse Core Ops, SparseCore 0:
  9.7 21.0 all-gather.3
  36.0 21.2 reduce-scatter.3
  136.5 6.8 reduce-scatter.5
  144.7 81.7 all-gather.7
Sparse Core Ops, SparseCore 1:
  39.2 78.1 all-gather.5
  248.7 135.8 reduce-scatter.7
where the time goes:
time: 398 us
  waiting for transfers between devices  250 us (63%)
  blocking collectives  87.2 us (22%)
  matrix products  32.3 us (8%)
  between operations  14.7 us (4%)
  local copies, waits for them, and re-layouts  7.4 us (2%)
  other arithmetic  6.04 us (2%)
    reduce_scatter x1, waiting for transfers between devices, shards(): lax.psum_scatter(lax.dot_general(mixed, basis_block, (((0,), (1,)), ((),...  136 us
    psum x1, blocking collectives, shards(): rotated_out = lax.psum(partial_out, ('tp', 'row')).astype(jnp.bfloat16)  85.1 us
    all_gather x1, waiting for transfers between devices, shards(): mixed = lax.all_gather(mixed, 'row', axis=0, tiled=True)  83.2 us
    all_gather x1, waiting for transfers between devices, shards(): basis_block = lax.all_gather(basis_in, 'col', axis=0, tiled=True)  22.6 us
    dot_general x1, matrix products, shards(): lax.dot_general(mixed, basis_block, (((0,), (1,)), ((), ())), preferred_e...  22 us
  transfers between devices with their start and end apart: 6, of which 4 were waited for; matrix products, arithmetic and copies ran while one was open for 0% of the time, Pallas kernels for 0%

commit v1 on v0

--- a/solution.py
+++ b/solution.py
@@ -29,7 +29,11 @@
     rotated_in = lax.all_gather(rotated_in, "col", axis=0, tiled=True)
     queries = rotated_in.shape[0]
     partial_out = jnp.dot(out_grad, basis_out, preferred_element_type=jnp.float32)
-    rotated_out = lax.psum(partial_out, ("tp", "row")).astype(jnp.bfloat16)
+
+    def detail_the_figure(in_array, axis_key, which_axis):
+        return lax.psum(lax.psum(in_array, axis_name=axis_key), axis_name=which_axis)
+
+    rotated_out = detail_the_figure(partial_out, "row", which_axis="tp").astype(jnp.bfloat16)
     coeff = contract_rows(rotated_in, rotated_out)
     scaled = (coeff / (queries * (eigen + damping))).astype(jnp.bfloat16)
     mixed_part = contract_cols(scaled, lax.all_gather(basis_out, ("tp", "row"), axis=0, tiled=True))

time: 398 us -> 421 us (1.058)
  waiting for transfers between devices: 250 us -> 335 us
  blocking collectives: 87.2 us -> 22.9 us
    all_gather x1, waiting for transfers between devices: 0.01 us -> 74.3 us  [shards(): lax.all_gather(basis_out, ('tp', 'row'), axis=0, tiled=True)]
    psum x1, blocking collectives: 85.1 us -> 20.8 us  [detail_the_figure(): lax.psum(lax.psum(in_array, axis_name=axis_key), axis_name=which_axis)]
    psum x0 -> x1, waiting for transfers between devices: none -> 12.6 us  [detail_the_figure(): lax.psum(in_array, axis_name=axis_key)]
  transfers between devices with their start and end apart: 6 -> 7, of which waited for: 4 -> 7; matrix products, arithmetic and copies ran while one was open for 0% -> 2% of each run, Pallas kernels for 0% -> 0%
where the time goes in v1:
time: 421 us
  waiting for transfers between devices  335 us (80%)
  matrix products  33.9 us (8%)
  blocking collectives  22.9 us (5%)
  between operations  14.9 us (4%)
  local copies, waits for them, and re-layouts  7.4 us (2%)
  other arithmetic  6.04 us (1%)
    reduce_scatter x1, waiting for transfers between devices, shards(): lax.psum_scatter(lax.dot_general(mixed, basis_block, (((0,), (1,)), ((),...  136 us
    all_gather x1, waiting for transfers between devices, shards(): mixed = lax.all_gather(mixed, 'row', axis=0, tiled=True)  81.7 us
    all_gather x1, waiting for transfers between devices, shards(): lax.all_gather(basis_out, ('tp', 'row'), axis=0, tiled=True)  74.3 us
    dot_general x1, matrix products, shards(): lax.dot_general(mixed, basis_block, (((0,), (1,)), ((), ())), preferred_e...  22 us
    psum x1, blocking collectives, detail_the_figure(): lax.psum(lax.psum(in_array, axis_name=axis_key), axis_name=which_axis)  20.8 us
    all_gather x1, waiting for transfers between devices, shards(): basis_block = lax.all_gather(basis_in, 'col', axis=0, tiled=True)  20.7 us
    psum x1, waiting for transfers between devices, detail_the_figure(): lax.psum(in_array, axis_name=axis_key)  12.6 us
    reduce_scatter x1, waiting for transfers between devices, shards(): lax.psum_scatter(mixed_part.astype(jnp.bfloat16), 'col', scatter_dimensio...  8.46 us
  transfers between devices with their start and end apart: 7, of which 7 were waited for; matrix products, arithmetic and copies ran while one was open for 2% of the time, Pallas kernels for 0%

profile of v1, /device:TPU:0, one launch (start us, length us, event | category | flops | bytes accessed | tf_op | source)
XLA Modules:
  0.0 420.8 jit_solution(7065538336549004446)
XLA Ops:
  7.4 0.0 copy-start
  7.4 0.0 all-gather.4.cloned.1.call-start
  7.4 0.7 all-gather.4.cloned.1.call-update
  8.1 0.0 all-reduce.3.cloned.1.call-start
  8.1 1.9 fusion.9
  10.0 0.0 all-reduce.3.cloned.1.call-update
  10.0 0.0 copy-start.1
  10.1 0.0 reduce-scatter.4.cloned.1.call-start
  10.1 20.7 %all-gather.4.cloned.1.call-done = bf16[3584,1024]{1,0:T(8,128)(2,1)} async-done(((bf16[1792,1024]{1,0:T(8,128)(2,1)}), bf16[3584,1024]{1,0:T(8,128)(2,1)}) %all-gather.4.cloned.1.call-update) | async-done | bytes 7340048 | tf_op jit(solution)/shard_map/all_gather | solution.py:24
  30.8 0.0 copy-done
  30.8 5.1 %convolution_convert_fusion.2 = bf16[64,1024]{1,0:T(8,128)(2,1)} fusion(bf16[64,3584]{1,0:T(8,128)(2,1)S(1)} %copy-done, bf16[3584,1024]{1,0:T(8,128)(2,1)} %all-gather.4.cloned.1.call-done), kind=kOutput, calls=%fused_computation.4 | convolution fusion | flops 469827584 | bytes 7929856 | tf_op jit(solution)/shard_map/dot_general | solution.py:25
  35.9 0.0 reduce-scatter.4.cloned.1.call-update
  35.9 0.0 all-gather.6.cloned.1.call-start
  36.0 0.5 all-gather.6.cloned.1.call-update
  36.5 0.0 reduce-scatter.6.cloned.1.call-start
  36.6 12.6 %all-reduce.3.cloned.1.call-done = f32[128,512]{1,0:T(8,128)} async-done(((f32[128,512]{1,0:T(8,128)}), f32[128,512]{1,0:T(8,128)}) %all-reduce.3.cloned.1.call-update) | async-done | bytes 262160 | tf_op jit(solution)/shard_map/psum | solution.py:34
  49.2 20.8 %all-reduce.4 = bf16[128,512]{1,0:T(8,128)(2,1)S(1)} all-reduce(f32[128,512]{1,0:T(8,128)} %all-reduce.3.cloned.1.call-done), channel_id=1, replica_groups=mesh['tp'=4,'row'=4,'col'=2] {'tp'}, use_global_device_ids=true, to_apply=%region_2.0 | all-reduce | flops 65536 | bytes 393216 | tf_op jit(solution)/shard_map/psum | solution.py:34
  70.0 0.2 reduce-scatter.4.cloned.1.call-done
  70.3 2.1 all_gather.13
  72.3 74.3 %all-gather.6.cloned.1.call-done = bf16[4096,512]{1,0:T(8,128)(2,1)} async-done(((bf16[256,512]{1,0:T(8,128)(2,1)}), bf16[4096,512]{1,0:T(8,128)(2,1)}) %all-gather.6.cloned.1.call-update) | async-done | bytes 4194320 | tf_op jit(solution)/shard_map/all_gather | solution.py:39
  146.6 0.0 copy-done.1
  146.6 4.9 %convolution_convert_fusion.1 = bf16[256,4096]{1,0:T(8,128)(2,1)} fusion(bf16[4096,512]{1,0:T(8,128)(2,1)} %all-gather.6.cloned.1.call-done, bf16[128,256]{1,0:T(8,128)(2,1)S(1)} %all_gather.13, f32[256,512]{1,0:T(8,128)S(1)} %copy-done.1, bf16[128,512]{1,0:T(8,128)(2,1)S(1)} %all-reduce.4), kind=kOutput, calls=%fused_computation.1 | convolution fusion | flops 1108869120 | bytes 7012352 | tf_op jit(solution)/shard_map/dot_general | solution.py:16
  151.5 3.3 convert_element_type.30
  154.8 4.1 copy.6
  158.9 0.0 reduce-scatter.6.cloned.1.call-update
  158.9 0.0 all-gather.8.cloned.1.call-start
  159.0 8.5 %reduce-scatter.6.cloned.1.call-done = bf16[256,4,1,512]{0,3,1,2:T(8,128)(2,1)} async-done(((bf16[256,4,2,512]{0,3,1,2:T(8,128)(2,1)}), bf16[256,4,1,512]{0,3,1,2:T(8,128)(2,1)}) %reduce-scatter.6.cloned.1.call-update) | async-done | bytes 1048592 | tf_op jit(solution)/shard_map/reduce_scatter | solution.py:43
  167.5 0.0 all-gather.8.cloned.1.call-update
  167.5 0.0 reduce-scatter.8.cloned.1.call-start
  167.5 81.7 %all-gather.8.cloned.1.call-done = bf16[1024,2048]{0,1:T(8,128)(2,1)} async-done(((bf16[256,2048]{0,1:T(8,128)(2,1)}), bf16[1024,2048]{0,1:T(8,128)(2,1)}) %all-gather.8.cloned.1.call-update) | async-done | bytes 4194320 | tf_op jit(solution)/shard_map/all_gather | solution.py:47
  249.3 22.0 %convolution_convert_fusion = bf16[2048,3584]{1,0:T(8,128)(2,1)} fusion(bf16[1024,2048]{0,1:T(8,128)(2,1)} %all-gather.8.cloned.1.call-done, bf16[3584,1024]{1,0:T(8,128)(2,1)} %all-gather.4.cloned.1.call-done), kind=kOutput, calls=%fused_computation | convolution fusion | flops 15039725568 | bytes 26214400 | tf_op jit(solution)/shard_map/dot_general | solution.py:49
  271.3 0.0 reduce-scatter.8.cloned.1.call-update
  271.3 136.1 %reduce-scatter.8.cloned.1.call-done = bf16[512,3584]{1,0:T(8,128)(2,1)} async-done(((bf16[2048,3584]{1,0:T(8,128)(2,1)}), bf16[512,3584]{1,0:T(8,128)(2,1)}) %reduce-scatter.8.cloned.1.call-update) | async-done | bytes 3670032 | tf_op jit(solution)/shard_map/reduce_scatter | solution.py:48
  407.4 6.0 %convert_element_type.33 = f32[512,3584]{1,0:T(8,128)} convert(bf16[512,3584]{1,0:T(8,128)(2,1)} %reduce-scatter.8.cloned.1.call-done) | non-fusion elementwise | flops 1835008 | bytes 11010048 | tf_op jit(solution)/shard_map/convert_element_type | solution.py:55
Async XLA Ops:
  7.4 23.4 %copy-start = (bf16[64,3584]{1,0:T(8,128)(2,1)S(1)}, bf16[64,3584]{1,0:T(8,128)(2,1)}, u32[]{:S(2)}) copy-start(bf16[64,3584]{1,0:T(8,128)(2,1)} %param.5) | copy-start | bytes 1376260
  7.4 23.4 %all-gather.4.cloned.1.call-start = ((), (), s32[]{:S(2)}) async-start(), calls=%async_computation.3 | async-start | bytes 11010048 | tf_op jit(solution)/shard_map/all_gather | solution.py:24
  8.1 41.1 %all-reduce.3.cloned.1.call-start = ((), (), s32[]{:S(2)}) async-start(), calls=%async_computation.5 | async-start | bytes 524288 | tf_op jit(solution)/shard_map/psum | solution.py:34
  10.0 136.5 %copy-start.1 = (f32[256,512]{1,0:T(8,128)S(1)}, f32[256,512]{1,0:T(8,128)}, u32[]{:S(2)}) copy-start(f32[256,512]{1,0:T(8,128)} %param.9) | copy-start | bytes 1572868
  10.1 60.2 %reduce-scatter.4.cloned.1.call-start = ((), (), s32[]{:S(2)}) async-start(), calls=%async_computation.4 | async-start | bytes 163840 | tf_op jit(solution)/shard_map/reduce_scatter | solution.py:26
  35.9 110.7 %all-gather.6.cloned.1.call-start = ((), (), s32[]{:S(2)}) async-start(), calls=%async_computation.6 | async-start | bytes 4456448 | tf_op jit(solution)/shard_map/all_gather | solution.py:39
  36.5 131.0 %reduce-scatter.6.cloned.1.call-start = ((), (), s32[]{:S(2)}) async-start(), calls=%async_computation.7 | async-start | bytes 3145728 | tf_op jit(solution)/shard_map/reduce_scatter | solution.py:43
  158.9 90.3 %all-gather.8.cloned.1.call-start = ((), (), s32[]{:S(2)}) async-start(), calls=%async_computation.8 | async-start | bytes 5242880 | tf_op jit(solution)/shard_map/all_gather | solution.py:47
  167.5 239.9 %reduce-scatter.8.cloned.1.call-start = ((), (), s32[]{:S(2)}) async-start(), calls=%async_computation.9 | async-start | bytes 18350080 | tf_op jit(solution)/shard_map/reduce_scatter | solution.py:48
Sparse Core Ops, SparseCore 0:
  9.7 21.0 all-gather.3
  159.1 8.3 reduce-scatter.5
  271.4 135.9 reduce-scatter.7
Sparse Core Ops, SparseCore 1:
  10.9 38.2 all-reduce.2
  51.3 18.9 reduce-scatter.3
  72.9 73.6 all-gather.5
  167.6 81.6 all-gather.7
